TPU v7x, 128 devices: a whole 4x4x4 slice. The times are simulated.
128 devices in a mesh: row: 8 (over y, x_hi), col: 16 (over z, x_lo, core).
Axes of the slice: x: 4 (x_hi: 2, x_lo: 2; x = x_hi * 2 + x_lo), y: 4, z: 4, core: 2. Of those that a mesh axis runs over, the one named last changes fastest.
Arguments:
- scen_inverse: bfloat16 [256, 512, 512], P(('row', 'col')), may hold values from -32 to 32, as said below
- coupling: bfloat16 [256, 512, 3072], P(('row', 'col')), may hold values from -0.0625 to 0.0625
- scen_cot: bfloat16 [256, 512, 256], P(('row', 'col')), may hold values from -6 to 6
- first_cot: float32 [3072, 256], P('row'), may hold values from -6 to 6
- schur_inverse: float32 [3072, 3072], P('row', 'col'), may hold values from -32 to 32, as said below
- scen_primal: bfloat16 [256, 512, 256], P(('row', 'col')), may hold values from -0.375 to 0.375
- first_primal: bfloat16 [3072, 256], replicated, may hold values from -0.375 to 0.375
Outputs:
- scen_adjoint: float32 [256, 512, 256], P(('row', 'col'))
- first_adjoint: float32 [3072, 256], P('col')
- coupling_grad: float32 [256, 512, 3072], P(('row', 'col'))
Inputs may be any that keep to these rules, and one draw needn't show every extreme that they name: `scen_inverse`: each block is full rank and well conditioned. `schur_inverse`: full rank and well conditioned.
All inputs are finite; a program needn't handle non-finite values.
Results may differ from a plain program's by a relative error of at most 0.005.
Values may be sent and summed in bfloat16 or wider, within the bound.
A program may use at most 128 MiB of HBM per device.

v0:
```python
import jax
import jax.numpy as jnp
from jax import lax
from jax.sharding import PartitionSpec as P


def cut_along(array, dim, size):
    dims = array.shape
    blocks = array.reshape(*dims[:dim], size, dims[dim] // size, *dims[dim + 1 :])
    return jnp.moveaxis(blocks, dim, 0)


def summed_on_arrival(array, axis, dim):
    size = lax.axis_size(axis)
    blocks = lax.all_to_all(cut_along(array, dim, size), axis, 0, 0, tiled=True)
    return jnp.sum(blocks, axis=0)


def gathered_total(array, axis):
    blocks = lax.all_gather(array, axis)
    return blocks.sum(axis=0)


def from_everyone(array, axis):
    size = lax.axis_size(axis)
    return lax.all_to_all(
        jnp.broadcast_to(array[None], (size, *array.shape)), axis, 0, 0, tiled=True
    )


def of_everyone(array, axis):
    everything = from_everyone(array, axis)
    return jnp.sum(everything, axis=0)


def body(scen_inverse, coupling, scen_cot, first_cot, schur_inverse, scen_primal, first_primal):
    helper = jnp.einsum(
        "smk,smr->skr", scen_inverse, scen_cot, preferred_element_type=jnp.float32
    ).astype(jnp.bfloat16)
    piece = summed_on_arrival(
        jnp.einsum("smn,smr->nr", coupling, helper, preferred_element_type=jnp.float32), "row", 0
    )
    block = gathered_total(piece, "col")
    condensed = first_cot - block
    tile_part = jnp.dot(
        schur_inverse.T,
        condensed,
        precision=lax.Precision.HIGHEST,
        preferred_element_type=jnp.float32,
    )
    first_adjoint = of_everyone(tile_part, "row")
    adjoint_low = lax.all_gather(first_adjoint.astype(jnp.bfloat16), "col", axis=0, tiled=True)
    update = (
        scen_cot.astype(jnp.float32)
        - jnp.einsum("smn,nr->smr", coupling, adjoint_low, preferred_element_type=jnp.float32)
    ).astype(jnp.bfloat16)
    scen_adjoint = jnp.einsum(
        "smk,smr->skr", scen_inverse, update, preferred_element_type=jnp.float32
    )
    scen_low = scen_adjoint.astype(jnp.bfloat16)
    coupling_grad = -(
        jnp.einsum("smr,nr->smn", scen_low, first_primal, preferred_element_type=jnp.float32)
        + jnp.einsum("smr,nr->smn", scen_primal, adjoint_low, preferred_element_type=jnp.float32)
    )
    return (scen_adjoint, first_adjoint, coupling_grad)


def solution(mesh):
    return jax.shard_map(
        body,
        mesh=mesh,
        in_specs=(
            P(("row", "col"), None, None),
            P(("row", "col"), None, None),
            P(("row", "col"), None, None),
            P("row", None),
            P("row", "col"),
            P(("row", "col"), None, None),
            P(),
        ),
        out_specs=(P(("row", "col"), None, None), P("col", None), P(("row", "col"), None, None)),
        check_vma=False,
    )
```

profile of v0, /device:TPU:1, one launch (start us, length us, event | category | flops | bytes accessed | tf_op | source)
XLA Modules:
  0.0 197.4 jit_solution(13329485175026890739)
XLA Ops:
  7.2 0.0 copy-start
  7.2 0.0 all-gather.6.cloned.1.call-start
  7.2 7.3 %fusion.17 = f32[256,3072,1]{1,0,2:T(8,128)} fusion(bf16[2,512,3072]{2,1,0:T(8,128)(2,1)} %param.8, bf16[2,512,512]{2,1,0:T(8,128)(2,1)} %param.7, bf16[2,512,256]{2,1,0:T(8,128)(2,1)} %param.9), kind=kOutput, calls=%fused_computation.15 | convolution fusion | flops 1879310336 | bytes 11010048 | tf_op jit(solution)/shard_map/smn,smr->nr/dot_general | solution.py:41
  14.5 2.1 %copy.46 = f32[32,8,8,384]{3,2,0,1:T(8,128)S(1)} copy(f32[32,8,8,384]{3,2,1,0:T(8,128)} %bitcast.53) | data formatting | bytes 6291456 | tf_op jit(solution)/shard_map/reshape | solution.py:9
  16.6 0.0 copy-start.4
  16.6 46.3 %all_to_all.10 = f32[8,384,256]{1,2,0:T(8,128)} all-to-all(f32[8,384,256]{1,2,0:T(8,128)S(1)} %bitcast.51), channel_id=1, replica_groups=mesh['row'=8,'col'=16] {'row'}, dimensions={0} | all-to-all | bytes 6291456 | tf_op jit(solution)/shard_map/all_to_all | solution.py:15
  62.9 2.8 %reduce_sum.27 = f32[384,256]{0,1:T(8,128)} reduce(f32[8,384,256]{1,2,0:T(8,128)} %all_to_all.10, f32[]{:T(128)} %constant.0.clone.1), dimensions={0}, to_apply=%region_0.0 | reduce | flops 688128 | bytes 3538948 | tf_op jit(solution)/shard_map/reduce_sum | solution.py:16
  65.7 0.0 all-gather.6.cloned.1.call-update
  65.8 0.0 all-gather.4.cloned.1.call-start
  65.8 0.0 copy-done.4
  65.8 0.2 copy.34
  66.0 42.3 %all-gather.6.cloned.1.call-done = f32[6144,256]{0,1:T(8,128)} async-done(((f32[384,256]{0,1:T(8,128)}), f32[6144,256]{0,1:T(8,128)}) %all-gather.6.cloned.1.call-update) | async-done | bytes 6291472 | tf_op jit(solution)/shard_map/all_gather | solution.py:20
  108.3 3.9 %copy.44 = f32[32,8,16,384]{3,2,1,0:T(8,128)S(1)} copy(f32[32,8,16,384]{3,1,2,0:T(8,128)} %bitcast.52) | data formatting | bytes 12582912
  112.2 0.0 copy-start.5
  112.2 1.5 bitcast_reduce_fusion
  113.7 0.0 copy-done.5
  113.7 0.6 convolution_bitcast_fusion.1
  114.3 0.1 broadcast_in_dim.2
  114.4 28.1 %all_to_all.11 = f32[8,192,256]{2,1,0:T(8,128)S(1)} all-to-all(f32[8,192,256]{2,1,0:T(8,128)S(1)} %broadcast_in_dim.2), channel_id=1, replica_groups=mesh['row'=8,'col'=16] {'row'}, dimensions={0} | all-to-all | bytes 3145728 | tf_op jit(solution)/shard_map/all_to_all | solution.py:26
  142.5 0.1 reduce_sum.29
  142.6 0.0 copy-start.2
  142.6 0.7 convert_element_type.17
  143.3 0.0 all-gather.4.cloned.1.call-update
  143.4 1.3 copy.29
  144.6 30.5 %all-gather.4.cloned.1.call-done = bf16[3072,256]{1,0:T(8,128)(2,1)} async-done(((bf16[192,256]{1,0:T(8,128)(2,1)}), bf16[3072,256]{1,0:T(8,128)(2,1)}) %all-gather.4.cloned.1.call-update) | async-done | bytes 1572880 | tf_op jit(solution)/shard_map/all_gather | solution.py:52
  175.1 5.6 %convolution_bitcast_fusion = f32[2,512,256]{1,2,0:T(8,128)S(1)} fusion(bf16[2,512,512]{2,1,0:T(8,128)(2,1)} %param.7, bf16[2,512,3072]{2,1,0:T(8,128)(2,1)} %param.8, bf16[3072,256]{1,0:T(8,128)(2,1)} %all-gather.4.cloned.1.call-done, bf16[2,512,256]{1,2,0:T(8,128)(2,1)S(1)} %copy.29), kind=kOutput, calls=%fused_computation.10 | convolution fusion | flops 1879834624 | bytes 10485760 | tf_op jit(solution)/shard_map/smk,smr->skr/dot_general | solution.py:57
  180.8 0.0 copy-done.2
  180.8 1.3 copy.37
  182.1 0.0 copy-done
  182.1 0.0 copy-start.1
  182.1 0.0 copy-start.3
  182.1 1.9 fusion.1
  183.9 0.0 copy-done.1
  183.9 0.0 copy-done.3
  184.0 6.6 %fusion = f32[2,512,3072]{2,1,0:T(8,128)} fusion(f32[2,512,3072]{2,1,0:T(8,128)S(1)} %fusion.1, bf16[2,512,256]{2,1,0:T(8,128)(2,1)S(1)} %copy-done.3, bf16[3072,256]{1,0:T(8,128)(2,1)S(1)} %copy-done.1), kind=kOutput, calls=%fused_computation.1 | convolution fusion | flops 1616904192 | bytes 27262976 | tf_op jit(solution)/shard_map/smr,nr->smn/dot_general | solution.py:63
Async XLA Ops:
  7.2 174.9 %copy-start = (bf16[3072,256]{1,0:T(8,128)(2,1)S(1)}, bf16[3072,256]{1,0:T(8,128)(2,1)}, u32[]{:S(2)}) copy-start(bf16[3072,256]{1,0:T(8,128)(2,1)} %param.13) | copy-start | bytes 4718596
  7.2 101.1 %all-gather.6.cloned.1.call-start = ((), (), s32[]{:S(2)}) async-start(), calls=%async_computation.3 | async-start | bytes 6684672 | tf_op jit(solution)/shard_map/all_gather | solution.py:20
  16.6 49.2 %copy-start.4 = (f32[384,256]{1,0:T(8,128)S(1)}, f32[384,256]{1,0:T(8,128)}, u32[]{:S(2)}) copy-start(f32[384,256]{1,0:T(8,128)} %param.10) | copy-start | bytes 1179652
  65.8 109.4 %all-gather.4.cloned.1.call-start = ((), (), s32[]{:S(2)}) async-start(), calls=%async_computation.2 | async-start | bytes 1671168 | tf_op jit(solution)/shard_map/all_gather | solution.py:52
  112.2 1.5 copy-start.5
  142.6 38.1 %copy-start.2 = (f32[192,256]{1,0:T(8,128)}, f32[192,256]{1,0:T(8,128)S(1)}, u32[]{:S(2)}) copy-start(f32[192,256]{1,0:T(8,128)S(1)} %reduce_sum.29) | copy-start | bytes 589828
  182.1 1.9 copy-start.1
  182.1 1.9 copy-start.3
Sparse Core Ops, SparseCore 0:
  65.9 42.3 all-gather.5
  143.5 31.6 all-gather.3
where the time goes:
time: 198 us; the launch traced here: 197 us
  blocking collectives  74.4 us (38%)
  waiting for transfers between devices  72.8 us (37%)
  matrix products  21.9 us (11%)
  between operations  14.2 us (7%)
  local copies, waits for them, and re-layouts  8.89 us (4%)
  other arithmetic  5.12 us (3%)
    all_to_all x1, blocking collectives, summed_on_arrival(): blocks = lax.all_to_all(cut_along(array, dim, size), axis, 0, 0, tiled=True)  46.3 us
    all_gather x1, waiting for transfers between devices, gathered_total(): blocks = lax.all_gather(array, axis)  42.3 us
    all_gather x1, waiting for transfers between devices, body(): lax.all_gather(first_adjoint.astype(jnp.bfloat16), 'col', axis=0, tiled=T...  30.5 us
    all_to_all x1, blocking collectives, from_everyone(): lax.all_to_all(jnp.broadcast_to(array[None], (size, *array.shape)), axis,...  28.1 us
    dot_general x1, matrix products, body(): jnp.einsum('smn,smr->nr', coupling, helper, preferred_element_type=jnp.fl...  7.26 us
    unnamed x16, local copies, waits for them, and re-layouts  6.67 us
    dot_general x1, matrix products, body(): jnp.einsum('smr,nr->smn', scen_primal, adjoint_low, preferred_element_typ...  6.61 us
    dot_general x1, matrix products, body(): jnp.einsum('smk,smr->skr', scen_inverse, update, preferred_element_type=j...  5.6 us
  transfers between devices with their start and end apart: 2, of which 2 were waited for; matrix products, arithmetic and copies ran while one was open for 1% of the time, Pallas kernels for 0%

commit v1 on v0

v1 whole, which is shorter than its diff:
```python
import functools

import jax
import jax.numpy as jnp
from jax import lax
from jax.experimental import pallas as pl
from jax.experimental.pallas import tpu as pltpu
from jax.sharding import PartitionSpec as P

MESH = pl.DeviceIdType.MESH
F32, BF16 = jnp.float32, jnp.bfloat16
FAR_FIRST = (2, 1, 3, 0)
NT = (((1,), (1,)), ((), ()))
TN = (((0,), (0,)), ((), ()))


def place():
    row, col = lax.axis_index("row"), lax.axis_index("col")
    return (row % 2) * 2 + (col // 2) % 2, row // 2, col // 4, col % 2


def device(x, y, z, core):
    return (y * 2 + x // 2, z * 4 + (x % 2) * 2 + core)


def part(start, size):
    return pl.ds(pl.multiple_of(start, size), size)


def wait_for(ref, sem):
    pltpu.make_async_copy(ref, ref, sem).wait()


def exchange(
    inverse_hbm, coupling_hbm, cot_hbm, first_hbm, schur_hbm,
    adjoint_hbm, q_ref,
    inverse, coupling, cot, first, schur, first_t, h_t, split,
    pair_send, pair_own, pair_recv, ring_send, ring_recv, plane_send, plane_recv,
    condensed, product, product_recv, adjoint,
    load_sem, chunk_sem, pair_ssem, pair_rsem, schur_ssem, schur_rsem, ring_ssem, ring_rsem,
    plane_ssem, plane_rsem, gather_ssem, gather_rsem, product_ssem, product_rsem,
    spread_ssem, spread_rsem, forward_ssem, forward_rsem, out_sem,
):
    x, y, z, core = place()
    x_hi, x_lo = x // 2, x % 2
    block, tile = y * 2 + x_hi, z * 2 + x_lo
    partner = device(x, y, z, 1 - core)

    def send(source, target, ssem, rsem, to):
        copy = pltpu.make_async_remote_copy(
            src_ref=source, dst_ref=target, send_sem=ssem, recv_sem=rsem, device_id=to, device_id_type=MESH
        )
        copy.start()

    barrier = pltpu.get_barrier_semaphore()
    for dx in range(4):
        for dy in range(4):
            for dz in range(4):
                if (dx, dy, dz) != (0, 0, 0):
                    there = device((x + dx) % 4, (y + dy) % 4, (z + dz) % 4, core)
                    pl.semaphore_signal(barrier, inc=1, device_id=there, device_id_type=MESH)
    pl.semaphore_signal(barrier, inc=1, device_id=partner, device_id_type=MESH)

    loads = [
        pltpu.make_async_copy(cot_hbm, cot, load_sem.at[0]),
        pltpu.make_async_copy(inverse_hbm, inverse, load_sem.at[1]),
    ]
    for copy in loads:
        copy.start()
    chunks = []
    for k, dy in enumerate(FAR_FIRST):
        lanes = part(((y + dy) % 4) * 768, 768)
        chunks.append(
            pltpu.make_async_copy(coupling_hbm.at[:, :, lanes], coupling.at[:, :, lanes], chunk_sem.at[k])
        )
        chunks[-1].start()
    late = [
        pltpu.make_async_copy(first_hbm, first, load_sem.at[2]),
        pltpu.make_async_copy(schur_hbm, schur.at[core], load_sem.at[3]),
    ]
    for copy in late:
        copy.start()

    for copy in loads:
        copy.wait()
    for s in range(2):
        helper = lax.dot_general(cot[s], inverse[s], TN, preferred_element_type=F32).astype(BF16)
        h_t[part((1 - core) * 128, 128), s * 512 : (s + 1) * 512] = helper[:128]
        h_t[part(core * 128, 128), s * 512 : (s + 1) * 512] = helper[128:]

    pl.semaphore_wait(barrier, 64)
    for copy in late:
        copy.wait()
    send(schur.at[core], schur.at[core], schur_ssem, schur_rsem, partner)

    def local_sum(k):
        lanes = part(((y + FAR_FIRST[k]) % 4) * 768, 768)
        chunks[k].wait()
        total = jnp.dot(h_t[:, :512], coupling[0, :, lanes], preferred_element_type=F32)
        total += jnp.dot(h_t[:, 512:], coupling[1, :, lanes], preferred_element_type=F32)
        pair_send[k] = total[:128].astype(BF16)
        pair_own[k] = total[128:]
        send(pair_send.at[k], pair_recv.at[k], pair_ssem, pair_rsem.at[k], partner)

    def to_ring(k):
        wait_for(pair_recv.at[k], pair_rsem.at[k])
        ring_send[k] = (pair_own[k] + pair_recv[k].astype(F32)).astype(BF16)
        for dx in (2, 1, 3):
            there = (x + dx) % 4
            send(
                ring_send.at[k, part((there % 2) * 64, 64), part((there // 2) * 384, 384)],
                ring_recv.at[dx - 1, k],
                ring_ssem,
                ring_rsem.at[dx - 1, k],
                device(there, y, z, core),
            )

    local_sum(0)
    for k in range(1, 4):
        local_sum(k)
        to_ring(k - 1)
    to_ring(3)

    first_t[...] = first[:, part(core * 128, 128)].T
    wait_for(schur.at[1 - core], schur_rsem)
    whole = schur[...].reshape(384, 384)
    high = whole.astype(BF16)
    split[0] = high
    split[1] = (whole - high.astype(F32)).astype(BF16)

    for k in range(4):
        total = ring_send[k, part(x_lo * 64, 64), part(x_hi * 384, 384)].astype(F32)
        for d in range(3):
            wait_for(ring_recv.at[d, k], ring_rsem.at[d, k])
            total += ring_recv[d, k].astype(F32)
        plane_send[k] = total.astype(BF16)
        for j, dz in enumerate(FAR_FIRST):
            if (k, j) != (3, 3):
                there = (z + dz) % 4
                send(
                    plane_send.at[k, part(there * 16, 16)],
                    plane_recv.at[k * 4 + j],
                    plane_ssem,
                    plane_rsem,
                    device(x, (y + FAR_FIRST[k]) % 4, there, core),
                )

    total = plane_send[3, part(z * 16, 16)].astype(F32)
    wait_for(plane_recv, plane_rsem)
    for k in range(15):
        total += plane_recv[k].astype(F32)
    slot = x_lo * 4 + z
    condensed[slot] = first_t[part(slot * 16, 16)] - total
    for dx in range(2):
        for dz in FAR_FIRST:
            if (dx, dz) != (0, 0):
                there = device(x_hi * 2 + (x_lo + dx) % 2, y, (z + dz) % 4, core)
                send(condensed.at[slot], condensed.at[slot], gather_ssem, gather_rsem, there)
    wait_for(condensed.at[pl.ds(0, 7)], gather_rsem)

    rows = condensed[...].reshape(128, 384)
    high = rows.astype(BF16)
    low = (rows - high.astype(F32)).astype(BF16)
    result = lax.dot_general(high, split[0], NT, preferred_element_type=F32)
    result += lax.dot_general(high, split[1], NT, preferred_element_type=F32)
    result += lax.dot_general(low, split[0], NT, preferred_element_type=F32)
    product[...] = result.reshape(8, 16, 384)
    for dy in FAR_FIRST:
        for dx in range(2):
            if (dx, dy) != (0, 0):
                there_y, there_x = (y + dy) % 4, (x_hi + dx) % 2
                send(
                    product.at[there_y * 2 + there_x],
                    product_recv.at[dy * 2 + dx - 1],
                    product_ssem,
                    product_rsem,
                    device(there_x * 2 + x_lo, there_y, z, core),
                )
    total = product[block]
    wait_for(product_recv, product_rsem)
    for k in range(7):
        total += product_recv[k]

    def spot(x, y, z):
        return adjoint.at[part(core * 128 + (y * 2 + x // 2) * 16, 16), part((z * 2 + x % 2) * 384, 384)]

    mine = spot(x, y, z)
    mine[...] = total.astype(BF16)
    send(mine, mine, forward_ssem, forward_rsem, partner)
    shifts = [(dx, dy, dz) for dx in FAR_FIRST for dy in FAR_FIRST for dz in FAR_FIRST][:63]
    for n, (dx, dy, dz) in enumerate(shifts):
        there = device((x + dx) % 4, (y + dy) % 4, (z + dz) % 4, core)
        send(mine, mine, spread_ssem.at[n], spread_rsem.at[n], there)
    for n, (dx, dy, dz) in enumerate(shifts):
        got = spot((x - dx) % 4, (y - dy) % 4, (z - dz) % 4)
        wait_for(got, spread_rsem.at[n])
        send(got, got, forward_ssem, forward_rsem, partner)
    wait_for(adjoint.at[part((1 - core) * 128, 128)], forward_rsem)
    out = pltpu.make_async_copy(adjoint, adjoint_hbm, out_sem)
    out.start()
    for s in range(2):
        took = lax.dot_general(coupling[s], adjoint[...], NT, preferred_element_type=F32)
        q_ref[s] = (cot[s].astype(F32) - took).astype(BF16)
    out.wait()

    wait_for(schur.at[core], schur_ssem)
    wait_for(pair_send, pair_ssem)
    wait_for(ring_recv, ring_ssem)
    wait_for(plane_recv, plane_ssem)
    wait_for(condensed.at[pl.ds(0, 7)], gather_ssem)
    wait_for(product_recv, product_ssem)
    for n in range(63):
        wait_for(mine, spread_ssem.at[n])
    wait_for(adjoint.at[part(core * 128, 128)], forward_ssem)


def gradients(inverse, q, primal, first_primal, adjoint, columns, scen_ref, first_ref, grad_ref, left):
    @pl.when(pl.program_id(0) == 0)
    def _():
        for s in range(2):
            value = lax.dot_general(inverse[s], q[s], TN, preferred_element_type=F32)
            scen_ref[s] = value
            left[s, :, :256] = -value.astype(BF16)
            left[s, :, 256:] = -primal[s]
        first_ref[...] = columns[...].astype(F32).T

    for s in range(2):
        grad = lax.dot_general(left[s, :, :256], first_primal[...], NT, preferred_element_type=F32)
        grad_ref[s] = grad + jnp.dot(left[s, :, 256:], adjoint[...], preferred_element_type=F32)


def body(scen_inverse, coupling, scen_cot, first_cot, schur_inverse, scen_primal, first_primal):
    any_space = pl.BlockSpec(memory_space=pl.ANY)
    dma = pltpu.SemaphoreType.DMA
    adjoint, q = pl.pallas_call(
        exchange,
        out_shape=(jax.ShapeDtypeStruct((256, 3072), BF16), jax.ShapeDtypeStruct((2, 512, 256), BF16)),
        in_specs=[any_space] * 5,
        out_specs=(any_space, pl.BlockSpec(memory_space=pltpu.VMEM)),
        scratch_shapes=[
            pltpu.VMEM((2, 512, 512), BF16),
            pltpu.VMEM((2, 512, 3072), BF16),
            pltpu.VMEM((2, 512, 256), BF16),
            pltpu.VMEM((384, 256), F32),
            pltpu.VMEM((2, 192, 384), F32),
            pltpu.VMEM((128, 384), F32),
            pltpu.VMEM((256, 1024), BF16),
            pltpu.VMEM((2, 384, 384), BF16),
            pltpu.VMEM((4, 128, 768), BF16),
            pltpu.VMEM((4, 128, 768), F32),
            pltpu.VMEM((4, 128, 768), BF16),
            pltpu.VMEM((4, 128, 768), BF16),
            pltpu.VMEM((3, 4, 64, 384), BF16),
            pltpu.VMEM((4, 64, 384), BF16),
            pltpu.VMEM((15, 16, 384), BF16),
            pltpu.VMEM((8, 16, 384), F32),
            pltpu.VMEM((8, 16, 384), F32),
            pltpu.VMEM((7, 16, 384), F32),
            pltpu.VMEM((256, 3072), BF16),
            dma((4,)), dma((4,)), dma, dma((4,)), dma, dma, dma, dma((3, 4)),
            dma, dma, dma, dma, dma, dma,
            dma((63,)), dma((63,)), dma, dma, dma,
        ],
        compiler_params=pltpu.CompilerParams(
            collective_id=0, has_side_effects=True, vmem_limit_bytes=40 * 1024 * 1024
        ),
        name="exchange",
    )(scen_inverse, coupling, scen_cot, first_cot, schur_inverse.T)
    column = lax.axis_index("col")
    columns = lax.dynamic_slice(adjoint, (0, column * 192), (256, 192))
    step = 256
    whole = lambda *shape: pl.BlockSpec(shape, lambda n: (0,) * len(shape), pipeline_mode=pl.Buffered(1))
    scen_adjoint, first_adjoint, coupling_grad = pl.pallas_call(
        gradients,
        out_shape=(
            jax.ShapeDtypeStruct((2, 512, 256), F32),
            jax.ShapeDtypeStruct((192, 256), F32),
            jax.ShapeDtypeStruct((2, 512, 3072), F32),
        ),
        grid=(3072 // step,),
        in_specs=[
            whole(2, 512, 512),
            whole(2, 512, 256),
            whole(2, 512, 256),
            pl.BlockSpec((step, 256), lambda n: (n, 0)),
            pl.BlockSpec((256, step), lambda n: (0, n)),
            whole(256, 192),
        ],
        out_specs=(
            whole(2, 512, 256),
            whole(192, 256),
            pl.BlockSpec((2, 512, step), lambda n: (0, 0, n)),
        ),
        scratch_shapes=[pltpu.VMEM((2, 512, 512), BF16)],
        compiler_params=pltpu.CompilerParams(vmem_limit_bytes=40 * 1024 * 1024),
        name="gradients",
    )(scen_inverse, q, scen_primal, first_primal, adjoint, columns)
    return scen_adjoint, first_adjoint, coupling_grad


def solution(mesh):
    return jax.shard_map(
        body,
        mesh=mesh,
        in_specs=(
            P(("row", "col"), None, None),
            P(("row", "col"), None, None),
            P(("row", "col"), None, None),
            P("row", None),
            P("row", "col"),
            P(("row", "col"), None, None),
            P(),
        ),
        out_specs=(P(("row", "col"), None, None), P("col", None), P(("row", "col"), None, None)),
        check_vma=False,
    )
```

time: 198 us -> 69.8 us (0.35)
  blocking collectives: 74.4 us -> 0 us
  waiting for transfers between devices: 72.8 us -> 0 us
  Pallas kernels: 0 us -> 61.7 us
  matrix products: 21.9 us -> 0 us
  between operations: 14.2 us -> 0.68 us
  other arithmetic: 5.12 us -> 0 us
    all_to_all x2 -> x0, blocking collectives: 74.4 us -> none  [the longest x1 46.3 us: summed_on_arrival(): blocks = lax.all_to_all(cut_along(array, dim, size), axis, 0, 0, tiled=True)]
    all_gather x2 -> x0, waiting for transfers between devices: 72.8 us -> none  [the longest x1 42.3 us: gathered_total(): blocks = lax.all_gather(array, axis)]
    pallas_call x0 -> x2, Pallas kernels: none -> 61.7 us  [the longest x1 51.9 us: body(): pl.pallas_call(exchange, out_shape=(jax.ShapeDtypeStruct((256, 3072), BF1...]
    dot_general x5 -> x0, matrix products: 21.9 us -> none  [the longest x1 7.26 us: body(): jnp.einsum('smn,smr->nr', coupling, helper, preferred_element_type=jnp.fl...]
    reduce_sum x3 -> x0, other arithmetic: 4.41 us -> none  [the longest x1 2.83 us: summed_on_arrival(): return jnp.sum(blocks, axis=0)]
    reshape x1 -> x0, local copies, waits for them, and re-layouts: 2.09 us -> none  [cut_along(): array.reshape(*dims[:dim], size, dims[dim] // size, *dims[dim + 1:])]
    unnamed x16 -> x14, local copies, waits for them, and re-layouts: 6.67 us -> 7.01 us
  transfers between devices with their start and end apart: 2 -> 0, of which waited for: 2 -> 0; matrix products, arithmetic and copies ran while one was open for 1% -> 0% of each run, Pallas kernels for 0% -> 0%
where the time goes in v1:
time: 69.8 us; the launch traced here: 69.5 us
  Pallas kernels  61.7 us (88%)
  local copies, waits for them, and re-layouts  7.12 us (10%)
    pallas_call x1, Pallas kernels, body(): pl.pallas_call(exchange, out_shape=(jax.ShapeDtypeStruct((256, 3072), BF1...  51.9 us
    pallas_call x1, Pallas kernels, body(): pl.pallas_call(gradients, out_shape=(jax.ShapeDtypeStruct((2, 512, 256),...  9.78 us
    unnamed x14, local copies, waits for them, and re-layouts  7.01 us

profile of v1, /device:TPU:1, one launch (start us, length us, event | category | flops | bytes accessed | tf_op | source)
XLA Modules:
  0.0 69.5 jit_solution(11174508747249428106)
XLA Ops:
  0.6 0.0 copy-start
  0.6 2.8 %copy-done = bf16[2,512,3072]{2,1,0:T(8,128)(2,1)S(1)} copy-done((bf16[2,512,3072]{2,1,0:T(8,128)(2,1)S(1)}, bf16[2,512,3072]{2,1,0:T(8,128)(2,1)}, u32[]{:S(2)}) %copy-start) | copy-done | bytes 6291480
  3.4 0.0 copy-start.1
  3.4 1.2 %copy-done.1 = bf16[2,512,512]{2,1,0:T(8,128)(2,1)S(1)} copy-done((bf16[2,512,512]{2,1,0:T(8,128)(2,1)S(1)}, bf16[2,512,512]{2,1,0:T(8,128)(2,1)}, u32[]{:S(2)}) %copy-start.1) | copy-done | bytes 1048600
  4.6 0.0 copy-start.3
  4.7 1.0 %copy-done.3 = bf16[2,512,256]{2,1,0:T(8,128)(2,1)S(1)} copy-done((bf16[2,512,256]{2,1,0:T(8,128)(2,1)S(1)}, bf16[2,512,256]{2,1,0:T(8,128)(2,1)}, u32[]{:S(2)}) %copy-start.3) | copy-done | bytes 524312
  5.7 0.0 copy-start.5
  5.7 1.0 %copy-done.5 = f32[384,256]{1,0:T(8,128)S(1)} copy-done((f32[384,256]{1,0:T(8,128)S(1)}, f32[384,256]{1,0:T(8,128)}, u32[]{:S(2)}) %copy-start.5) | copy-done | bytes 393240
  6.7 0.0 copy-start.6
  6.7 1.0 %copy-done.6 = f32[384,192]{0,1:T(8,128)S(1)} copy-done((f32[384,192]{0,1:T(8,128)S(1)}, f32[384,192]{0,1:T(8,128)}, u32[]{:S(2)}) %copy-start.6) | copy-done | bytes 294936
  7.6 0.0 copy-start.2
  7.7 0.0 copy-start.4
  7.7 51.9 %exchange.1 = (bf16[256,3072]{1,0:T(8,128)(2,1)S(1)}, bf16[2,512,256]{2,1,0:T(8,128)(2,1)S(1)}) custom-call(bf16[2,512,512]{2,1,0:T(8,128)(2,1)S(1)} %copy-done.1, bf16[2,512,3072]{2,1,0:T(8,128)(2,1)S(1)} %copy-done, bf16[2,512,256]{2,1,0:T(8,128)(2,1)S(1)} %copy-done.3, f32[384,256]{1,0:T(8,128)S(1)} %copy-done.5, f32[192,384]{1,0:T(8,128)S(1)} %bitcast.1), custom_call_target="tpu_custom_call" | custom-call | tf_op jit(solution)/shard_map/exchange/pallas_call | solution.py:235
  59.6 0.1 constant_dynamic-slice_fusion.columns
  59.7 0.0 copy-done.2
  59.7 0.0 copy-done.4
  59.7 9.8 %gradients.1 = (f32[2,512,256]{2,1,0:T(8,128)}, f32[192,256]{1,0:T(8,128)}, f32[2,512,3072]{2,1,0:T(8,128)}) custom-call(bf16[2,512,512]{2,1,0:T(8,128)(2,1)S(1)} %copy-done.1, bf16[2,512,256]{2,1,0:T(8,128)(2,1)S(1)} %get-tuple-element.5.q, bf16[2,512,256]{2,1,0:T(8,128)(2,1)S(1)} %copy-done.4, bf16[3072,256]{1,0:T(8,128)(2,1)S(1)} %copy-done.2, ...), custom_call_target="tpu_custom_call" | custom-call | tf_op jit(solution)/shard_map/gradients/pallas_call | solution.py:273
Async XLA Ops:
  0.6 2.8 %copy-start = (bf16[2,512,3072]{2,1,0:T(8,128)(2,1)S(1)}, bf16[2,512,3072]{2,1,0:T(8,128)(2,1)}, u32[]{:S(2)}) copy-start(bf16[2,512,3072]{2,1,0:T(8,128)(2,1)} %coupling_hbm.1) | copy-start | bytes 18874372
  3.4 1.2 %copy-start.1 = (bf16[2,512,512]{2,1,0:T(8,128)(2,1)S(1)}, bf16[2,512,512]{2,1,0:T(8,128)(2,1)}, u32[]{:S(2)}) copy-start(bf16[2,512,512]{2,1,0:T(8,128)(2,1)} %inverse.1) | copy-start | bytes 3145732
  4.6 1.0 %copy-start.3 = (bf16[2,512,256]{2,1,0:T(8,128)(2,1)S(1)}, bf16[2,512,256]{2,1,0:T(8,128)(2,1)}, u32[]{:S(2)}) copy-start(bf16[2,512,256]{2,1,0:T(8,128)(2,1)} %cot_hbm.1) | copy-start | bytes 1572868
  5.7 1.0 %copy-start.5 = (f32[384,256]{1,0:T(8,128)S(1)}, f32[384,256]{1,0:T(8,128)}, u32[]{:S(2)}) copy-start(f32[384,256]{1,0:T(8,128)} %first_hbm.1) | copy-start | bytes 1179652
  6.7 1.0 %copy-start.6 = (f32[384,192]{0,1:T(8,128)S(1)}, f32[384,192]{0,1:T(8,128)}, u32[]{:S(2)}) copy-start(f32[384,192]{0,1:T(8,128)} %param.11) | copy-start | bytes 884740
  7.6 52.1 %copy-start.2 = (bf16[3072,256]{1,0:T(8,128)(2,1)S(1)}, bf16[3072,256]{1,0:T(8,128)(2,1)}, u32[]{:S(2)}) copy-start(bf16[3072,256]{1,0:T(8,128)(2,1)} %first_primal.1) | copy-start | bytes 4718596
  7.7 52.1 %copy-start.4 = (bf16[2,512,256]{2,1,0:T(8,128)(2,1)S(1)}, bf16[2,512,256]{2,1,0:T(8,128)(2,1)}, u32[]{:S(2)}) copy-start(bf16[2,512,256]{2,1,0:T(8,128)(2,1)} %primal.1) | copy-start | bytes 1572868

commit v2 on v1

v2 whole, which is shorter than its diff:
```python
import functools

import jax
import jax.numpy as jnp
from jax import lax
from jax.experimental import pallas as pl
from jax.experimental.pallas import tpu as pltpu
from jax.sharding import PartitionSpec as P

MESH = pl.DeviceIdType.MESH
F32, BF16 = jnp.float32, jnp.bfloat16
FAR_FIRST = (2, 1, 3, 0)
NT = (((1,), (1,)), ((), ()))
TN = (((0,), (0,)), ((), ()))


def place():
    row, col = lax.axis_index("row"), lax.axis_index("col")
    return (row % 2) * 2 + (col // 2) % 2, row // 2, col // 4, col % 2


def device(x, y, z, core):
    return (y * 2 + x // 2, z * 4 + (x % 2) * 2 + core)


def part(start, size):
    return pl.ds(pl.multiple_of(start, size), size)


def wait_for(ref, sem):
    pltpu.make_async_copy(ref, ref, sem).wait()


def exchange(
    inverse_hbm, coupling_hbm, cot_hbm, first_hbm, schur_hbm, primal_hbm,
    adjoint_hbm, scen_ref, left_ref,
    inverse, inverse_t, coupling, cot, primal, first, schur, first_t, h_t, split,
    pair_send, pair_own, pair_recv, ring_send, ring_recv, plane_send, plane_recv,
    condensed, product, product_recv, adjoint, taken,
    load_sem, chunk_sem, near_sem, pair_ssem, pair_rsem, schur_ssem, schur_rsem, ring_ssem, ring_rsem,
    plane_ssem, plane_rsem, gather_ssem, gather_rsem, product_ssem, product_rsem,
    spread_ssem, spread_rsem, forward_ssem, forward_rsem, out_sem,
):
    x, y, z, core = place()
    x_hi, x_lo = x // 2, x % 2
    block, tile = y * 2 + x_hi, z * 2 + x_lo
    partner = device(x, y, z, 1 - core)
    drains = []

    def finish():
        for ref, sem in drains:
            wait_for(ref, sem)

    def send(source, target, ssem, rsem, to):
        copy = pltpu.make_async_remote_copy(
            src_ref=source, dst_ref=target, send_sem=ssem, recv_sem=rsem, device_id=to, device_id_type=MESH
        )
        copy.start()

    barrier = pltpu.get_barrier_semaphore()
    rings = [device((x + d) % 4, y, z, core) for d in (1, 2, 3)]
    y_ring = [device(x, (y + d) % 4, z, core) for d in (1, 2, 3)]
    rings += y_ring + [device(x, y, (z + d) % 4, core) for d in (1, 2, 3)]
    for there in rings + [partner]:
        pl.semaphore_signal(barrier, inc=1, device_id=there, device_id_type=MESH)

    loads = [
        pltpu.make_async_copy(cot_hbm, cot, load_sem.at[0]),
        pltpu.make_async_copy(inverse_hbm, inverse, load_sem.at[1]),
    ]
    for copy in loads:
        copy.start()
    chunks = []
    for k, dy in enumerate(FAR_FIRST):
        lanes = part(((y + dy) % 4) * 768, 768)
        chunks.append(
            pltpu.make_async_copy(coupling_hbm.at[:, :, lanes], coupling.at[:, :, lanes], chunk_sem.at[k])
        )
        chunks[-1].start()
    late = [
        pltpu.make_async_copy(first_hbm, first, load_sem.at[2]),
        pltpu.make_async_copy(schur_hbm, schur.at[core], load_sem.at[3]),
        pltpu.make_async_copy(primal_hbm, primal, load_sem.at[4]),
    ]
    for copy in late:
        copy.start()

    for copy in loads:
        copy.wait()
    for s in range(2):
        helper = lax.dot_general(cot[s], inverse[s], TN, preferred_element_type=F32).astype(BF16)
        h_t[part((1 - core) * 128, 128), s * 512 : (s + 1) * 512] = helper[:128]
        h_t[part(core * 128, 128), s * 512 : (s + 1) * 512] = helper[128:]

    def local_sum(k):
        lanes = part(((y + FAR_FIRST[k]) % 4) * 768, 768)
        chunks[k].wait()
        total = jnp.dot(h_t[:, :512], coupling[0, :, lanes], preferred_element_type=F32)
        total += jnp.dot(h_t[:, 512:], coupling[1, :, lanes], preferred_element_type=F32)
        pair_send[k] = total[:128].astype(BF16)
        pair_own[k] = total[128:]

    def to_pair(k):
        send(pair_send.at[k], pair_recv.at[k], pair_ssem, pair_rsem.at[k], partner)

    def to_ring(k):
        wait_for(pair_recv.at[k], pair_rsem.at[k])
        ring_send[k] = (pair_own[k] + pair_recv[k].astype(F32)).astype(BF16)
        for dx in (2, 1, 3):
            there = (x + dx) % 4
            send(
                ring_send.at[k, part((there % 2) * 64, 64), part((there // 2) * 384, 384)],
                ring_recv.at[dx - 1, k],
                ring_ssem,
                ring_rsem.at[dx - 1, k],
                device(there, y, z, core),
            )

    drains.append((pair_send, pair_ssem))
    drains.append((ring_recv, ring_ssem))
    local_sum(0)
    pl.semaphore_wait(barrier, 10)
    to_pair(0)
    for there in y_ring:
        pl.semaphore_signal(near_sem, inc=1, device_id=there, device_id_type=MESH)
    for k in range(1, 4):
        local_sum(k)
        to_pair(k)
        to_ring(k - 1)
    for copy in late:
        copy.wait()
    send(schur.at[core], schur.at[core], schur_ssem, schur_rsem, partner)
    drains.append((schur.at[core], schur_ssem))
    to_ring(3)

    pl.semaphore_wait(near_sem, 3)
    drains.append((plane_recv, plane_ssem))
    for k in range(4):
        total = ring_send[k, part(x_lo * 64, 64), part(x_hi * 384, 384)].astype(F32)
        for d in range(3):
            wait_for(ring_recv.at[d, k], ring_rsem.at[d, k])
            total += ring_recv[d, k].astype(F32)
        plane_send[k] = total.astype(BF16)
        for j, dz in enumerate(FAR_FIRST):
            if (k, j) != (3, 3):
                there = (z + dz) % 4
                send(
                    plane_send.at[k, part(there * 16, 16)],
                    plane_recv.at[k * 4 + j],
                    plane_ssem,
                    plane_rsem,
                    device(x, (y + FAR_FIRST[k]) % 4, there, core),
                )

    first_t[...] = first[:, part(core * 128, 128)].T
    wait_for(schur.at[1 - core], schur_rsem)
    whole = schur[...].reshape(384, 384)
    high = whole.astype(BF16)
    split[0] = high
    split[1] = (whole - high.astype(F32)).astype(BF16)
    total = plane_send[3, part(z * 16, 16)].astype(F32)
    wait_for(plane_recv, plane_rsem)
    for k in range(15):
        total += plane_recv[k].astype(F32)
    slot = x_lo * 4 + z
    condensed[slot] = first_t[part(slot * 16, 16)] - total
    drains.append((condensed.at[pl.ds(0, 7)], gather_ssem))
    for dx in (1, 0):
        for dz in FAR_FIRST:
            if (dx, dz) != (0, 0):
                there = device(x_hi * 2 + (x_lo + dx) % 2, y, (z + dz) % 4, core)
                send(condensed.at[slot], condensed.at[slot], gather_ssem, gather_rsem, there)
    inverse_t[0] = inverse[0].T
    inverse_t[1] = inverse[1].T
    wait_for(condensed.at[pl.ds(0, 7)], gather_rsem)

    rows = condensed[...].reshape(128, 384)
    high = rows.astype(BF16)
    low = (rows - high.astype(F32)).astype(BF16)
    result = lax.dot_general(high, split[0], NT, preferred_element_type=F32)
    result += lax.dot_general(high, split[1], NT, preferred_element_type=F32)
    result += lax.dot_general(low, split[0], NT, preferred_element_type=F32)
    product[...] = result.reshape(8, 16, 384)
    drains.append((product_recv, product_ssem))
    for dx in (1, 0):
        for dy in FAR_FIRST:
            if (dx, dy) != (0, 0):
                there_y, there_x = (y + dy) % 4, (x_hi + dx) % 2
                send(
                    product.at[there_y * 2 + there_x],
                    product_recv.at[dy * 2 + dx - 1],
                    product_ssem,
                    product_rsem,
                    device(there_x * 2 + x_lo, there_y, z, core),
                )
    for s in range(2):
        left_ref[s, :, 256:] = -primal[s]
    total = product[block]
    wait_for(product_recv, product_rsem)
    for k in range(7):
        total += product_recv[k]

    def spot(x, y, z):
        return adjoint.at[part(core * 128 + (y * 2 + x // 2) * 16, 16), part((z * 2 + x % 2) * 384, 384)]

    mine = spot(x, y, z)
    mine[...] = total.astype(BF16)
    shifts = [(dx, dy, dz) for dz in FAR_FIRST for dx in FAR_FIRST for dy in FAR_FIRST][:63]
    for n, (dx, dy, dz) in enumerate(shifts):
        there = device((x + dx) % 4, (y + dy) % 4, (z + dz) % 4, core)
        send(mine, mine, spread_ssem.at[n], spread_rsem.at[n], there)
        drains.append((mine, spread_ssem.at[n]))
    send(mine, mine, forward_ssem, forward_rsem.at[3], partner)

    def take(group):
        lanes = part(((z - FAR_FIRST[group]) % 4) * 768, 768)
        theirs = adjoint.at[part((1 - core) * 128, 128), lanes]
        wait_for(theirs, forward_rsem.at[group])
        for s in range(2):
            term = lax.dot_general(coupling[s, :, lanes], adjoint[:, lanes], NT, preferred_element_type=F32)
            if group == 0:
                taken[s] = term
            else:
                taken[s] += term

    for group in range(4):
        for n in range(group * 16, min(group * 16 + 16, 63)):
            dx, dy, dz = shifts[n]
            got = spot((x - dx) % 4, (y - dy) % 4, (z - dz) % 4)
            wait_for(got, spread_rsem.at[n])
            send(got, got, forward_ssem, forward_rsem.at[group], partner)
        if group:
            take(group - 1)
    drains.append((adjoint.at[part(core * 128, 128)], forward_ssem))
    wait_for(adjoint.at[part((1 - core) * 128, 128), part(z * 768, 768)], forward_rsem.at[3])
    out = pltpu.make_async_copy(adjoint, adjoint_hbm, out_sem)
    out.start()
    lanes = part(z * 768, 768)
    for s in range(2):
        term = lax.dot_general(coupling[s, :, lanes], adjoint[:, lanes], NT, preferred_element_type=F32)
        q = (cot[s].astype(F32) - (taken[s] + term)).astype(BF16)
        value = jnp.dot(inverse_t[s], q, preferred_element_type=F32)
        scen_ref[s] = value
        left_ref[s, :, :256] = -value.astype(BF16)
    out.wait()
    finish()


STEP = 256


def gradients(left, first_primal, adjoint, scen, columns, scen_hbm, first_ref, grad_hbm, buffer, scen_sem, sems):
    scen_copy = pltpu.make_async_copy(scen, scen_hbm, scen_sem)
    scen_copy.start()

    def write(n):
        return pltpu.make_async_copy(
            buffer.at[n % 3], grad_hbm.at[:, :, part(n * STEP, STEP)], sems.at[n % 3]
        )

    def step(n, carry):
        @pl.when(n >= 3)
        def _():
            write(n - 3).wait()

        at = part(n * STEP, STEP)
        for s in range(2):
            grad = lax.dot_general(left[s, :, :256], first_primal[at], NT, preferred_element_type=F32)
            buffer[n % 3, s] = grad + jnp.dot(left[s, :, 256:], adjoint[:, at], preferred_element_type=F32)
        write(n).start()
        return carry

    steps = 3072 // STEP
    lax.fori_loop(0, steps, step, 0)
    first_ref[...] = columns[...].astype(F32).T
    for n in range(steps - 3, steps):
        write(n).wait()
    scen_copy.wait()


def body(scen_inverse, coupling, scen_cot, first_cot, schur_inverse, scen_primal, first_primal):
    any_space, vmem = pl.BlockSpec(memory_space=pl.ANY), pl.BlockSpec(memory_space=pltpu.VMEM)
    dma = pltpu.SemaphoreType.DMA
    operands = (scen_inverse, coupling, scen_cot, first_cot, schur_inverse.T, scen_primal)
    adjoint, scen, left = pl.pallas_call(
        exchange,
        out_shape=(
            jax.ShapeDtypeStruct((256, 3072), BF16),
            jax.ShapeDtypeStruct((2, 512, 256), F32),
            jax.ShapeDtypeStruct((2, 512, 512), BF16),
        ),
        in_specs=[any_space] * 6,
        out_specs=(any_space, vmem, vmem),
        scratch_shapes=[
            pltpu.VMEM((2, 512, 512), BF16),
            pltpu.VMEM((2, 512, 512), BF16),
            pltpu.VMEM((2, 512, 3072), BF16),
            pltpu.VMEM((2, 512, 256), BF16),
            pltpu.VMEM((2, 512, 256), BF16),
            pltpu.VMEM((384, 256), F32),
            pltpu.VMEM((2, 192, 384), F32),
            pltpu.VMEM((128, 384), F32),
            pltpu.VMEM((256, 1024), BF16),
            pltpu.VMEM((2, 384, 384), BF16),
            pltpu.VMEM((4, 128, 768), BF16),
            pltpu.VMEM((4, 128, 768), F32),
            pltpu.VMEM((4, 128, 768), BF16),
            pltpu.VMEM((4, 128, 768), BF16),
            pltpu.VMEM((3, 4, 64, 384), BF16),
            pltpu.VMEM((4, 64, 384), BF16),
            pltpu.VMEM((15, 16, 384), BF16),
            pltpu.VMEM((8, 16, 384), F32),
            pltpu.VMEM((8, 16, 384), F32),
            pltpu.VMEM((7, 16, 384), F32),
            pltpu.VMEM((256, 3072), BF16),
            pltpu.VMEM((2, 512, 256), F32),
            dma((5,)), dma((4,)), pltpu.SemaphoreType.REGULAR, dma, dma((4,)), dma, dma, dma, dma((3, 4)),
            dma, dma, dma, dma, dma, dma,
            dma((63,)), dma((63,)), dma, dma((4,)), dma,
        ],
        compiler_params=pltpu.CompilerParams(
            collective_id=0, has_side_effects=True, vmem_limit_bytes=36 * 1024 * 1024
        ),
        name="exchange",
    )(*(pltpu.with_memory_space_constraint(array, pltpu.HBM) for array in operands))
    columns = lax.dynamic_slice(adjoint, (0, lax.axis_index("col") * 192), (256, 192))
    return pl.pallas_call(
        gradients,
        out_shape=(
            jax.ShapeDtypeStruct((2, 512, 256), F32),
            jax.ShapeDtypeStruct((192, 256), F32),
            jax.ShapeDtypeStruct((2, 512, 3072), F32),
        ),
        in_specs=[vmem] * 5,
        out_specs=(any_space, vmem, any_space),
        scratch_shapes=[pltpu.VMEM((3, 2, 512, STEP), F32), dma, dma((3,))],
        compiler_params=pltpu.CompilerParams(vmem_limit_bytes=24 * 1024 * 1024),
        name="gradients",
    )(left, first_primal, adjoint, scen, columns)


def solution(mesh):
    return jax.shard_map(
        body,
        mesh=mesh,
        in_specs=(
            P(("row", "col"), None, None),
            P(("row", "col"), None, None),
            P(("row", "col"), None, None),
            P("row", None),
            P("row", "col"),
            P(("row", "col"), None, None),
            P(),
        ),
        out_specs=(P(("row", "col"), None, None), P("col", None), P(("row", "col"), None, None)),
        check_vma=False,
    )
```

time: 69.8 us -> 57.7 us (0.83)
  local copies, waits for them, and re-layouts: 7.12 us -> 0.12 us
  Pallas kernels: 61.7 us -> 56.8 us
    unnamed x14 -> x2, local copies, waits for them, and re-layouts: 7.01 us -> 0.01 us
    pallas_call x1, Pallas kernels: 9.78 us -> 7.27 us  [body(): pl.pallas_call(gradients, out_shape=(jax.ShapeDtypeStruct((2, 512, 256),...]
    pallas_call x1, Pallas kernels: 51.9 us -> 49.5 us  [body(): pl.pallas_call(exchange, out_shape=(jax.ShapeDtypeStruct((256, 3072), BF1...]
where the time goes in v2:
time: 57.7 us; the launch traced here: 57.6 us
  Pallas kernels  56.8 us (98%)
  between operations  0.67 us (1%)
    pallas_call x1, Pallas kernels, body(): pl.pallas_call(exchange, out_shape=(jax.ShapeDtypeStruct((256, 3072), BF1...  49.5 us
    pallas_call x1, Pallas kernels, body(): pl.pallas_call(gradients, out_shape=(jax.ShapeDtypeStruct((2, 512, 256),...  7.27 us

profile of v2, /device:TPU:1, one launch (start us, length us, event | category | flops | bytes accessed | tf_op | source)
XLA Modules:
  0.0 57.6 jit_solution(15003446587765959328)
XLA Ops:
  0.6 0.0 copy-start
  0.6 49.5 %exchange.1 = (bf16[256,3072]{1,0:T(8,128)(2,1)S(1)}, f32[2,512,256]{2,1,0:T(8,128)S(1)}, bf16[2,512,512]{2,1,0:T(8,128)(2,1)S(1)}) custom-call(bf16[2,512,512]{2,1,0:T(8,128)(2,1)} %inverse_hbm.1, bf16[2,512,3072]{2,1,0:T(8,128)(2,1)} %coupling_hbm.1, bf16[2,512,256]{2,1,0:T(8,128)(2,1)} %cot_hbm.1, f32[384,256]{1,0:T(8,128)} %first_hbm.1, ...), custom_call_target="tpu_custom_call" | custom-call | tf_op jit(solution)/shard_map/exchange/pallas_call | solution.py:285
  50.2 0.1 constant_dynamic-slice_fusion.columns
  50.3 0.0 copy-done
  50.3 7.3 %gradients.1 = (f32[2,512,256]{2,1,0:T(8,128)}, f32[192,256]{1,0:T(8,128)}, f32[2,512,3072]{2,1,0:T(8,128)}) custom-call(bf16[2,512,512]{2,1,0:T(8,128)(2,1)S(1)} %get-tuple-element.6.left, bf16[3072,256]{1,0:T(8,128)(2,1)S(1)} %copy-done, bf16[256,3072]{1,0:T(8,128)(2,1)S(1)} %get-tuple-element.7.adjoint, f32[2,512,256]{2,1,0:T(8,128)S(1)} %get-tuple-element.8.scen, ...), custom_call_target="tpu_custom_call" | custom-call | tf_op jit(solution)/shard_map/gradients/pallas_call | solution.py:327
Async XLA Ops:
  0.6 49.7 %copy-start = (bf16[3072,256]{1,0:T(8,128)(2,1)S(1)}, bf16[3072,256]{1,0:T(8,128)(2,1)}, u32[]{:S(2)}) copy-start(bf16[3072,256]{1,0:T(8,128)(2,1)} %first_primal.1) | copy-start | bytes 4718596

commit v3 on v2

v3 whole, which is shorter than its diff:
```python
import functools

import jax
import jax.numpy as jnp
from jax import lax
from jax.experimental import pallas as pl
from jax.experimental.pallas import tpu as pltpu
from jax.sharding import PartitionSpec as P

MESH = pl.DeviceIdType.MESH
F32, BF16 = jnp.float32, jnp.bfloat16
FAR_FIRST = (2, 1, 3, 0)
NT = (((1,), (1,)), ((), ()))
TN = (((0,), (0,)), ((), ()))


def place():
    row, col = lax.axis_index("row"), lax.axis_index("col")
    return (row % 2) * 2 + (col // 2) % 2, row // 2, col // 4, col % 2


def device(x, y, z, core):
    return (y * 2 + x // 2, z * 4 + (x % 2) * 2 + core)


def part(start, size):
    return pl.ds(pl.multiple_of(start, size), size)


def wait_for(ref, sem):
    pltpu.make_async_copy(ref, ref, sem).wait()


def exchange(
    inverse_hbm, coupling_hbm, cot_hbm, first_hbm, schur_hbm, primal_hbm, base_hbm,
    scen_ref, left_ref, right_ref,
    inverse, inverse_t, coupling, cot, primal, base, first, schur, first_t, h_t, split,
    pair_send, pair_own, pair_recv, ring_send, ring_recv, plane_send, plane_recv,
    condensed, product, product_recv, adjoint, taken,
    load_sem, chunk_sem, pair_ssem, pair_rsem, schur_ssem, schur_rsem,
    near_sem, ring_ssem, ring_rsem, plane_ssem, plane_rsem,
    gather_ssem, gather_rsem, product_ssem, product_rsem,
    spread_ssem, spread_rsem, forward_ssem, forward_rsem, out_sem,
):
    x, y, z, core = place()
    x_hi, x_lo = x // 2, x % 2
    block, tile = y * 2 + x_hi, z * 2 + x_lo
    partner = device(x, y, z, 1 - core)
    drains = []

    def finish():
        for ref, sem in drains:
            wait_for(ref, sem)

    def send(source, target, ssem, rsem, to):
        copy = pltpu.make_async_remote_copy(
            src_ref=source, dst_ref=target, send_sem=ssem, recv_sem=rsem, device_id=to, device_id_type=MESH
        )
        copy.start()

    loads = [
        pltpu.make_async_copy(cot_hbm, cot, load_sem.at[0]),
        pltpu.make_async_copy(inverse_hbm, inverse, load_sem.at[1]),
    ]
    for copy in loads:
        copy.start()
    chunks = []
    for k, dy in enumerate(FAR_FIRST):
        lanes = part(((y + dy) % 4) * 768, 768)
        chunks.append(
            pltpu.make_async_copy(coupling_hbm.at[:, :, lanes], coupling.at[:, :, lanes], chunk_sem.at[k])
        )
    chunks[0].start()
    chunks[1].start()

    here = (x, y, z)

    def moved(*steps):
        spot = [(c + d) % 4 for c, d in zip(here, steps)]
        return device(*spot, core)

    barrier = pltpu.get_barrier_semaphore()
    x_ring = [moved(d, 0, 0) for d in (1, 2, 3)]
    y_ring = [moved(0, d, 0) for d in (1, 2, 3)]
    z_ring = [moved(0, 0, d) for d in (1, 2, 3)]
    for there in x_ring + y_ring + z_ring + [partner]:
        pl.semaphore_signal(barrier, inc=1, device_id=there, device_id_type=MESH)

    late = [
        pltpu.make_async_copy(first_hbm, first, load_sem.at[2]),
        pltpu.make_async_copy(schur_hbm, schur.at[core], load_sem.at[3]),
        pltpu.make_async_copy(primal_hbm, primal, load_sem.at[4]),
        pltpu.make_async_copy(base_hbm, base, load_sem.at[5]),
    ]
    for copy in loads:
        copy.wait()
    for copy in chunks[2:] + late:
        copy.start()
    for s in range(2):
        helper = lax.dot_general(cot[s], inverse[s], TN, preferred_element_type=F32).astype(BF16)
        h_t[part((1 - core) * 128, 128), s * 512 : (s + 1) * 512] = helper[:128]
        h_t[part(core * 128, 128), s * 512 : (s + 1) * 512] = helper[128:]

    def local_sum(k):
        lanes = part(((y + FAR_FIRST[k]) % 4) * 768, 768)
        chunks[k].wait()
        total = jnp.dot(h_t[...], coupling[:, :, lanes].reshape(1024, 768), preferred_element_type=F32)
        pair_send[k] = total[:128].astype(BF16)
        pair_own[k] = total[128:]

    def to_pair(k):
        send(pair_send.at[k], pair_recv.at[k], pair_ssem, pair_rsem.at[k], partner)

    def to_rings(k):
        wait_for(pair_recv.at[k], pair_rsem.at[k])
        there_y = (y + FAR_FIRST[k]) % 4
        total = (pair_own[k] + pair_recv[k].astype(F32)).astype(BF16)
        for hi in range(2):
            for lo in range(2):
                column = hi * 2 + lo
                for p in range(3):
                    lane = hi * 384 + p * 128
                    tiles = total[lo * 64 : lo * 64 + 64, lane : lane + 128].reshape(4, 16, 128)
                    if p == 0:
                        ring_send[0, column, there_y] = tiles
                    elif p == 1:
                        ring_send[1, there_y, column] = tiles
                    else:
                        ring_send[2, :, there_y, column] = tiles
        for d in (2, 1, 3):
            for p, own in ((0, x), (2, z)):
                send(
                    ring_send.at[p, (own + d) % 4, there_y],
                    ring_recv.at[p, d - 1, there_y],
                    ring_ssem.at[p],
                    ring_rsem.at[p, d - 1],
                    (x_ring if p == 0 else z_ring)[d - 1],
                )
        d = FAR_FIRST[k]
        if d:
            send(ring_send.at[1, there_y], ring_recv.at[1, d - 1], ring_ssem.at[1], ring_rsem.at[1, d - 1], y_ring[d - 1])

    drains.append((pair_send, pair_ssem))
    for p in range(3):
        drains.append((ring_recv.at[p], ring_ssem.at[p]))
    local_sum(0)
    pl.semaphore_wait(barrier, 10)
    to_pair(0)
    for there in x_ring + y_ring:
        pl.semaphore_signal(near_sem, inc=1, device_id=there, device_id_type=MESH)
    local_sum(1)
    to_pair(1)
    to_rings(0)
    local_sum(2)
    to_pair(2)
    to_rings(1)
    local_sum(3)
    to_pair(3)
    to_rings(2)
    to_rings(3)

    pl.semaphore_wait(near_sem, 6)
    drains.append((plane_recv.at[:, pl.ds(1, 15)], plane_ssem))
    for p, own, u, v in ((1, y, x, z), (0, x, y, z), (2, z, y, x)):
        total = ring_send[p, own].astype(F32)
        for d in range(3):
            wait_for(ring_recv.at[p, d], ring_rsem.at[p, d])
            total += ring_recv[p, d].astype(F32)
        plane_send[p] = total.astype(BF16)
        for du in FAR_FIRST:
            for dv in FAR_FIRST:
                if (du, dv) != (0, 0):
                    there = moved(*((0, du, dv), (du, 0, dv), (dv, du, 0))[p])
                    send(
                        plane_send.at[p, (u + du) % 4, (v + dv) % 4],
                        plane_recv.at[p, du * 4 + dv],
                        plane_ssem,
                        plane_rsem.at[p],
                        there,
                    )
        plane_recv[p, 0] = plane_send[p, u, v]

    for copy in late:
        copy.wait()
    send(schur.at[core], schur.at[core], schur_ssem, schur_rsem, partner)
    drains.append((schur.at[core], schur_ssem))
    for n in range(0, 3072, 768):
        right_ref[:256, n : n + 768] = base[n : n + 768].T
    first_t[...] = first[:, part(core * 128, 128)].T
    wait_for(schur.at[1 - core], schur_rsem)
    whole = schur[...].reshape(384, 384)
    high = whole.astype(BF16)
    split[0] = high
    split[1] = (whole - high.astype(F32)).astype(BF16)
    slot = x_lo * 4 + z
    for p in (1, 0, 2):
        lanes = slice(p * 128, p * 128 + 128)
        wait_for(plane_recv.at[p, pl.ds(1, 15)], plane_rsem.at[p])
        condensed[slot, :, lanes] = first_t[part(slot * 16, 16), lanes] - jnp.sum(plane_recv[p].astype(F32), axis=0)
    drains.append((condensed.at[pl.ds(0, 7)], gather_ssem))
    for dx in (1, 0):
        for dz in FAR_FIRST:
            if (dx, dz) != (0, 0):
                there = device(x_hi * 2 + (x_lo + dx) % 2, y, (z + dz) % 4, core)
                send(condensed.at[slot], condensed.at[slot], gather_ssem, gather_rsem, there)
    inverse_t[0] = inverse[0].T
    inverse_t[1] = inverse[1].T
    wait_for(condensed.at[pl.ds(0, 7)], gather_rsem)

    rows = condensed[...].reshape(128, 384)
    high = rows.astype(BF16)
    low = (rows - high.astype(F32)).astype(BF16)
    result = lax.dot_general(high, split[0], NT, preferred_element_type=F32)
    result += lax.dot_general(high, split[1], NT, preferred_element_type=F32)
    result += lax.dot_general(low, split[0], NT, preferred_element_type=F32)
    product[...] = result.astype(BF16).reshape(8, 16, 384)
    drains.append((product_recv, product_ssem))
    for dx in (1, 0):
        for dy in FAR_FIRST:
            if (dx, dy) != (0, 0):
                there_y, there_x = (y + dy) % 4, (x_hi + dx) % 2
                send(
                    product.at[there_y * 2 + there_x],
                    product_recv.at[dy * 2 + dx - 1],
                    product_ssem,
                    product_rsem,
                    device(there_x * 2 + x_lo, there_y, z, core),
                )
    for s in range(2):
        left_ref[s, :, 256:] = -primal[s]
    total = product[block].astype(F32)
    wait_for(product_recv, product_rsem)
    for k in range(7):
        total += product_recv[k].astype(F32)

    def spot(x, y, z):
        return adjoint.at[part(core * 128 + (y * 2 + x // 2) * 16, 16), part((z * 2 + x % 2) * 384, 384)]

    mine = spot(x, y, z)
    mine[...] = total.astype(BF16)
    spread = [(dx, dy, dz) for dz in FAR_FIRST for dx in FAR_FIRST for dy in FAR_FIRST][:63]
    for n, (dx, dy, dz) in enumerate(spread):
        there = device((x + dx) % 4, (y + dy) % 4, (z + dz) % 4, core)
        send(mine, mine, spread_ssem.at[n], spread_rsem.at[n], there)
        drains.append((mine, spread_ssem.at[n]))

    outs = []
    for group in range(4):
        lanes = part(((z - FAR_FIRST[group]) % 4) * 768, 768)
        outs.append(pltpu.make_async_copy(adjoint.at[:, lanes], right_ref.at[pl.ds(256, 256), lanes], out_sem.at[group]))

    def take(group):
        lanes = part(((z - FAR_FIRST[group]) % 4) * 768, 768)
        theirs = adjoint.at[part((1 - core) * 128, 128), lanes]
        wait_for(theirs, forward_rsem.at[group])
        outs[group].start()
        for s in range(2):
            term = lax.dot_general(coupling[s, :, lanes], adjoint[:, lanes], NT, preferred_element_type=F32)
            if group == 0:
                taken[s] = term
            else:
                taken[s] += term

    for group in range(4):
        for n in range(group * 16, min(group * 16 + 16, 63)):
            dx, dy, dz = spread[n]
            got = spot((x - dx) % 4, (y - dy) % 4, (z - dz) % 4)
            wait_for(got, spread_rsem.at[n])
        here = adjoint.at[part(core * 128, 128), part(((z - FAR_FIRST[group]) % 4) * 768, 768)]
        send(here, here, forward_ssem, forward_rsem.at[group], partner)
        if group:
            take(group - 1)
    drains.append((adjoint.at[part(core * 128, 128)], forward_ssem))
    wait_for(adjoint.at[part((1 - core) * 128, 128), part(z * 768, 768)], forward_rsem.at[3])
    outs[3].start()
    lanes = part(z * 768, 768)
    for s in range(2):
        term = lax.dot_general(coupling[s, :, lanes], adjoint[:, lanes], NT, preferred_element_type=F32)
        q = (cot[s].astype(F32) - (taken[s] + term)).astype(BF16)
        value = jnp.dot(inverse_t[s], q, preferred_element_type=F32)
        scen_ref[s] = value
        left_ref[s, :, :256] = -value.astype(BF16)
    for copy in outs:
        copy.wait()
    finish()


ROWS, SLOTS = 128, 4


def gradients(left, right, scen, columns, scen_hbm, first_ref, grad_hbm, buffer, scen_sem, sems):
    scen_copy = pltpu.make_async_copy(scen, scen_hbm, scen_sem)
    scen_copy.start()

    def write(n):
        rows = pl.ds(n * ROWS % 512, ROWS)
        return pltpu.make_async_copy(buffer.at[n % SLOTS], grad_hbm.at[n * ROWS // 512, rows], sems.at[n % SLOTS])

    steps = 1024 // ROWS
    for n in range(steps):
        if n >= SLOTS:
            write(n - SLOTS).wait()
        rows = pl.ds(n * ROWS % 512, ROWS)
        buffer[n % SLOTS] = jnp.dot(left[n * ROWS // 512, rows], right[...], preferred_element_type=F32)
        write(n).start()
    first_ref[...] = columns[...].astype(F32).T
    for n in range(steps - SLOTS, steps):
        write(n).wait()
    scen_copy.wait()


def body(scen_inverse, coupling, scen_cot, first_cot, schur_inverse, scen_primal, first_primal):
    any_space, vmem = pl.BlockSpec(memory_space=pl.ANY), pl.BlockSpec(memory_space=pltpu.VMEM)
    dma = pltpu.SemaphoreType.DMA
    operands = (scen_inverse, coupling, scen_cot, first_cot, schur_inverse.T, scen_primal, first_primal)
    scen, left, right = pl.pallas_call(
        exchange,
        out_shape=(
            jax.ShapeDtypeStruct((2, 512, 256), F32),
            jax.ShapeDtypeStruct((2, 512, 512), BF16),
            jax.ShapeDtypeStruct((512, 3072), BF16),
        ),
        in_specs=[any_space] * 7,
        out_specs=(vmem, vmem, vmem),
        scratch_shapes=[
            pltpu.VMEM((2, 512, 512), BF16),
            pltpu.VMEM((2, 512, 512), BF16),
            pltpu.VMEM((2, 512, 3072), BF16),
            pltpu.VMEM((2, 512, 256), BF16),
            pltpu.VMEM((2, 512, 256), BF16),
            pltpu.VMEM((3072, 256), BF16),
            pltpu.VMEM((384, 256), F32),
            pltpu.VMEM((2, 192, 384), F32),
            pltpu.VMEM((128, 384), F32),
            pltpu.VMEM((256, 1024), BF16),
            pltpu.VMEM((2, 384, 384), BF16),
            pltpu.VMEM((4, 128, 768), BF16),
            pltpu.VMEM((4, 128, 768), F32),
            pltpu.VMEM((4, 128, 768), BF16),
            pltpu.VMEM((3, 4, 4, 4, 16, 128), BF16),
            pltpu.VMEM((3, 3, 4, 4, 16, 128), BF16),
            pltpu.VMEM((3, 4, 4, 16, 128), BF16),
            pltpu.VMEM((3, 16, 16, 128), BF16),
            pltpu.VMEM((8, 16, 384), F32),
            pltpu.VMEM((8, 16, 384), BF16),
            pltpu.VMEM((7, 16, 384), BF16),
            pltpu.VMEM((256, 3072), BF16),
            pltpu.VMEM((2, 512, 256), F32),
            dma((6,)), dma((4,)), dma, dma((4,)), dma, dma,
            pltpu.SemaphoreType.REGULAR, dma((3,)), dma((3, 3)), dma, dma((3,)),
            dma, dma, dma, dma,
            dma((63,)), dma((63,)), dma, dma((4,)), dma((4,)),
        ],
        compiler_params=pltpu.CompilerParams(
            collective_id=0, has_side_effects=True, vmem_limit_bytes=36 * 1024 * 1024
        ),
        name="exchange",
    )(*(pltpu.with_memory_space_constraint(array, pltpu.HBM) for array in operands))
    columns = lax.dynamic_slice(right, (256, lax.axis_index("col") * 192), (256, 192))
    return pl.pallas_call(
        gradients,
        out_shape=(
            jax.ShapeDtypeStruct((2, 512, 256), F32),
            jax.ShapeDtypeStruct((192, 256), F32),
            jax.ShapeDtypeStruct((2, 512, 3072), F32),
        ),
        in_specs=[vmem] * 4,
        out_specs=(any_space, vmem, any_space),
        scratch_shapes=[pltpu.VMEM((SLOTS, ROWS, 3072), F32), dma, dma((SLOTS,))],
        compiler_params=pltpu.CompilerParams(vmem_limit_bytes=24 * 1024 * 1024),
        name="gradients",
    )(left, right, scen, columns)


def solution(mesh):
    return jax.shard_map(
        body,
        mesh=mesh,
        in_specs=(
            P(("row", "col"), None, None),
            P(("row", "col"), None, None),
            P(("row", "col"), None, None),
            P("row", None),
            P("row", "col"),
            P(("row", "col"), None, None),
            P(),
        ),
        out_specs=(P(("row", "col"), None, None), P("col", None), P(("row", "col"), None, None)),
        check_vma=False,
    )
```

time: 57.7 us -> 52.4 us (0.908)
  Pallas kernels: 56.8 us -> 51.5 us
    pallas_call x1, Pallas kernels: 49.5 us -> 45.5 us  [body(): pl.pallas_call(exchange, out_shape=(jax.ShapeDtypeStruct((2, 512, 256), F...]
    pallas_call x1, Pallas kernels: 7.27 us -> 6.05 us  [body(): pl.pallas_call(gradients, out_shape=(jax.ShapeDtypeStruct((2, 512, 256),...]
where the time goes in v3:
time: 52.4 us; the launch traced here: 52.3 us
  Pallas kernels  51.5 us (98%)
  between operations  0.65 us (1%)
    pallas_call x1, Pallas kernels, body(): pl.pallas_call(exchange, out_shape=(jax.ShapeDtypeStruct((2, 512, 256), F...  45.5 us
    pallas_call x1, Pallas kernels, body(): pl.pallas_call(gradients, out_shape=(jax.ShapeDtypeStruct((2, 512, 256),...  6.05 us

profile of v3, /device:TPU:1, one launch (start us, length us, event | category | flops | bytes accessed | tf_op | source)
XLA Modules:
  0.0 52.3 jit_solution(15669432133430459392)
XLA Ops:
  0.6 45.5 %exchange.1 = (f32[2,512,256]{2,1,0:T(8,128)S(1)}, bf16[2,512,512]{2,1,0:T(8,128)(2,1)S(1)}, bf16[512,3072]{1,0:T(8,128)(2,1)S(1)}) custom-call(bf16[2,512,512]{2,1,0:T(8,128)(2,1)} %inverse_hbm.1, bf16[2,512,3072]{2,1,0:T(8,128)(2,1)} %coupling_hbm.1, bf16[2,512,256]{2,1,0:T(8,128)(2,1)} %cot_hbm.1, f32[384,256]{1,0:T(8,128)} %first_hbm.1, ...), custom_call_target="tpu_custom_call" | custom-call | tf_op jit(solution)/shard_map/exchange/pallas_call | solution.py:316
  46.1 0.1 constant_dynamic-slice_fusion.columns
  46.2 6.0 %gradients.1 = (f32[2,512,256]{2,1,0:T(8,128)}, f32[192,256]{1,0:T(8,128)}, f32[2,512,3072]{2,1,0:T(8,128)}) custom-call(bf16[2,512,512]{2,1,0:T(8,128)(2,1)S(1)} %get-tuple-element.6.left, bf16[512,3072]{1,0:T(8,128)(2,1)S(1)} %get-tuple-element.7.right, f32[2,512,256]{2,1,0:T(8,128)S(1)} %get-tuple-element.8.scen, ...), custom_call_target="tpu_custom_call" | custom-call | tf_op jit(solution)/shard_map/gradients/pallas_call | solution.py:360

commit v4 on v3

--- a/solution.py
+++ b/solution.py
@@ -58,10 +58,10 @@
         )
         copy.start()
 
-    loads = [
-        pltpu.make_async_copy(cot_hbm, cot, load_sem.at[0]),
-        pltpu.make_async_copy(inverse_hbm, inverse, load_sem.at[1]),
-    ]
+    loads = []
+    for s in range(2):
+        loads.append(pltpu.make_async_copy(cot_hbm.at[s], cot.at[s], load_sem.at[2 * s]))
+        loads.append(pltpu.make_async_copy(inverse_hbm.at[s], inverse.at[s], load_sem.at[2 * s + 1]))
     for copy in loads:
         copy.start()
     chunks = []
@@ -87,16 +87,15 @@
         pl.semaphore_signal(barrier, inc=1, device_id=there, device_id_type=MESH)
 
     late = [
-        pltpu.make_async_copy(first_hbm, first, load_sem.at[2]),
-        pltpu.make_async_copy(schur_hbm, schur.at[core], load_sem.at[3]),
-        pltpu.make_async_copy(primal_hbm, primal, load_sem.at[4]),
-        pltpu.make_async_copy(base_hbm, base, load_sem.at[5]),
+        pltpu.make_async_copy(first_hbm, first, load_sem.at[4]),
+        pltpu.make_async_copy(schur_hbm, schur.at[core], load_sem.at[5]),
+        pltpu.make_async_copy(primal_hbm, primal, load_sem.at[6]),
+        pltpu.make_async_copy(base_hbm, base, load_sem.at[7]),
     ]
-    for copy in loads:
-        copy.wait()
-    for copy in chunks[2:] + late:
-        copy.start()
     for s in range(2):
+        loads[2 * s].wait()
+        loads[2 * s + 1].wait()
+        chunks[2 + s].start()
         helper = lax.dot_general(cot[s], inverse[s], TN, preferred_element_type=F32).astype(BF16)
         h_t[part((1 - core) * 128, 128), s * 512 : (s + 1) * 512] = helper[:128]
         h_t[part(core * 128, 128), s * 512 : (s + 1) * 512] = helper[128:]
@@ -104,6 +103,9 @@
     def local_sum(k):
         lanes = part(((y + FAR_FIRST[k]) % 4) * 768, 768)
         chunks[k].wait()
+        if k == 3:
+            for copy in late:
+                copy.start()
         total = jnp.dot(h_t[...], coupling[:, :, lanes].reshape(1024, 768), preferred_element_type=F32)
         pair_send[k] = total[:128].astype(BF16)
         pair_own[k] = total[128:]
@@ -288,7 +290,7 @@
 ROWS, SLOTS = 128, 4
 
 
-def gradients(left, right, scen, columns, scen_hbm, first_ref, grad_hbm, buffer, scen_sem, sems):
+def gradients(left, right, scen, scen_hbm, first_ref, grad_hbm, buffer, tile, scen_sem, sems):
     scen_copy = pltpu.make_async_copy(scen, scen_hbm, scen_sem)
     scen_copy.start()
 
@@ -303,7 +305,9 @@
         rows = pl.ds(n * ROWS % 512, ROWS)
         buffer[n % SLOTS] = jnp.dot(left[n * ROWS // 512, rows], right[...], preferred_element_type=F32)
         write(n).start()
-    first_ref[...] = columns[...].astype(F32).T
+    column = lax.axis_index("col")
+    tile[...] = right[256:, part(column // 2 * 384, 384)].astype(F32).T
+    first_ref[...] = tile[part(column % 2 * 192, 192)]
     for n in range(steps - SLOTS, steps):
         write(n).wait()
     scen_copy.wait()
@@ -346,7 +350,7 @@
             pltpu.VMEM((7, 16, 384), BF16),
             pltpu.VMEM((256, 3072), BF16),
             pltpu.VMEM((2, 512, 256), F32),
-            dma((6,)), dma((4,)), dma, dma((4,)), dma, dma,
+            dma((8,)), dma((4,)), dma, dma((4,)), dma, dma,
             pltpu.SemaphoreType.REGULAR, dma((3,)), dma((3, 3)), dma, dma((3,)),
             dma, dma, dma, dma,
             dma((63,)), dma((63,)), dma, dma((4,)), dma((4,)),
@@ -356,7 +360,6 @@
         ),
         name="exchange",
     )(*(pltpu.with_memory_space_constraint(array, pltpu.HBM) for array in operands))
-    columns = lax.dynamic_slice(right, (256, lax.axis_index("col") * 192), (256, 192))
     return pl.pallas_call(
         gradients,
         out_shape=(
@@ -364,12 +367,12 @@
             jax.ShapeDtypeStruct((192, 256), F32),
             jax.ShapeDtypeStruct((2, 512, 3072), F32),
         ),
-        in_specs=[vmem] * 4,
+        in_specs=[vmem] * 3,
         out_specs=(any_space, vmem, any_space),
-        scratch_shapes=[pltpu.VMEM((SLOTS, ROWS, 3072), F32), dma, dma((SLOTS,))],
+        scratch_shapes=[pltpu.VMEM((SLOTS, ROWS, 3072), F32), pltpu.VMEM((384, 256), F32), dma, dma((SLOTS,))],
         compiler_params=pltpu.CompilerParams(vmem_limit_bytes=24 * 1024 * 1024),
         name="gradients",
-    )(left, right, scen, columns)
+    )(left, right, scen)
 
 
 def solution(mesh):

time: 52.4 us -> 52.1 us (level)
  no operation moved by 1% of the time
where the time goes in v4:
time: 52.1 us; the launch traced here: 52 us
  Pallas kernels  51.3 us (98%)
  between operations  0.64 us (1%)
    pallas_call x1, Pallas kernels, body(): pl.pallas_call(exchange, out_shape=(jax.ShapeDtypeStruct((2, 512, 256), F...  45.3 us
    pallas_call x1, Pallas kernels, body(): pl.pallas_call(gradients, out_shape=(jax.ShapeDtypeStruct((2, 512, 256),...  6.05 us

profile of v4, /device:TPU:1, one launch (start us, length us, event | category | flops | bytes accessed | tf_op | source)
XLA Modules:
  0.0 52.0 jit_solution(14625079028615297757)
XLA Ops:
  0.6 45.3 %exchange.1 = (f32[2,512,256]{2,1,0:T(8,128)S(1)}, bf16[2,512,512]{2,1,0:T(8,128)(2,1)S(1)}, bf16[512,3072]{1,0:T(8,128)(2,1)S(1)}) custom-call(bf16[2,512,512]{2,1,0:T(8,128)(2,1)} %inverse_hbm.1, bf16[2,512,3072]{2,1,0:T(8,128)(2,1)} %coupling_hbm.1, bf16[2,512,256]{2,1,0:T(8,128)(2,1)} %cot_hbm.1, f32[384,256]{1,0:T(8,128)} %first_hbm.1, ...), custom_call_target="tpu_custom_call" | custom-call | tf_op jit(solution)/shard_map/exchange/pallas_call | solution.py:320
  45.9 6.0 %gradients.1 = (f32[2,512,256]{2,1,0:T(8,128)}, f32[192,256]{1,0:T(8,128)}, f32[2,512,3072]{2,1,0:T(8,128)}) custom-call(bf16[2,512,512]{2,1,0:T(8,128)(2,1)S(1)} %get-tuple-element.6.left, bf16[512,3072]{1,0:T(8,128)(2,1)S(1)} %get-tuple-element.7.right, f32[2,512,256]{2,1,0:T(8,128)S(1)} %get-tuple-element.8.scen), custom_call_target="tpu_custom_call" | custom-call | tf_op jit(solution)/shard_map/gradients/pallas_call | solution.py:363
